TPU v7x, 32 devices: a whole 2x2x4 slice. The times are simulated.
32 devices in a mesh: fsdp: 4 (over y, core), ctx: 2 (over x), tp: 4 (over z).
Axes of the slice: x: 2, y: 2, z: 4, core: 2. Of those that a mesh axis runs over, the one named last changes fastest.
Arguments:
- hidden_in: bfloat16 [16, 1024, 768], P('fsdp', 'ctx'), may hold values from -6 to 6
- prev_logits: bfloat16 [16, 12, 1024, 1024], P('fsdp', 'tp', 'ctx'), may hold values from -6 to 6
- w_query: bfloat16 [768, 768], P('fsdp', 'tp'), may hold values from -0.21875 to 0.21875
- w_key: bfloat16 [768, 768], P('fsdp', 'tp'), may hold values from -0.21875 to 0.21875
- w_value: bfloat16 [768, 768], P('fsdp', 'tp'), may hold values from -0.21875 to 0.21875
- w_out: bfloat16 [768, 768], P('fsdp', 'tp'), may hold values from -1.75 to 1.75
- w_inner: bfloat16 [768, 3072], P('fsdp', 'tp'), may hold values from -0.21875 to 0.21875
- w_outer: bfloat16 [768, 3072], P('fsdp', 'tp'), may hold values from -0.109375 to 0.109375
- b_query: float32 [768], P('tp'), may hold values from -3 to 3
- b_value: float32 [768], P('tp'), may hold values from -3 to 3
- b_out: float32 [768], replicated, may hold values from -3 to 3
- b_inner: float32 [3072], P('tp'), may hold values from -3 to 3
- b_outer: float32 [768], replicated, may hold values from -3 to 3
- gain_attn: float32 [768], replicated, may hold values from 0.25 to 1.75
- shift_attn: float32 [768], replicated, may hold values from -3 to 3
- gain_ffn: float32 [768], replicated, may hold values from 0.25 to 1.75
- shift_ffn: float32 [768], replicated, may hold values from -3 to 3
- d_output: bfloat16 [16, 1024, 768], P('fsdp', 'ctx'), may hold values from -6 to 6
- d_logits: bfloat16 [16, 12, 1024, 1024], P('fsdp', 'tp', 'ctx'), may hold values from -6 to 6
Outputs:
- output: bfloat16 [16, 1024, 768], P('fsdp', 'ctx')
- new_logits: bfloat16 [16, 12, 1024, 1024], P('fsdp', 'tp', 'ctx')
- d_hidden: float32 [16, 1024, 768], P('fsdp', 'ctx')
- d_prev: bfloat16 [16, 12, 1024, 1024], P('fsdp', 'tp', 'ctx')
- d_w_query: float32 [768, 768], P('fsdp', 'tp')
- d_w_key: float32 [768, 768], P('fsdp', 'tp')
- d_w_value: float32 [768, 768], P('fsdp', 'tp')
- d_w_out: float32 [768, 768], P('fsdp', 'tp')
- d_w_inner: float32 [768, 3072], P('fsdp', 'tp')
- d_w_outer: float32 [768, 3072], P('fsdp', 'tp')
- d_b_query: float32 [768], P('tp')
- d_b_value: float32 [768], P('tp')
- d_b_out: float32 [768], replicated
- d_b_inner: float32 [3072], P('tp')
- d_b_outer: float32 [768], replicated
- d_gain_attn: float32 [768], replicated
- d_shift_attn: float32 [768], replicated
- d_gain_ffn: float32 [768], replicated
- d_shift_ffn: float32 [768], replicated
All inputs are finite; a program needn't handle non-finite values.
Results may differ from a plain program's by a relative error of at most 0.017.
Values may be sent and summed in bfloat16 or wider, within the bound.
No kernel may reach another device: no remote copies, remote signals or barrier semaphores. Data moves between devices by JAX's collectives and lax.ppermute only.
A program may use at most 448 MiB of HBM per device.

v0:
```python
import jax
import jax.numpy as jnp
from jax import lax
from jax.sharding import PartitionSpec as P

BLOCK = 256


def layer_norm(value, gain, shift):
    mean = jnp.mean(value, axis=-1, keepdims=True)
    centered = value - mean
    variance = jnp.mean(centered * centered, axis=-1, keepdims=True)
    return centered * lax.rsqrt(variance + 1e-06) * gain + shift


def gelu_exact(value):
    return jax.nn.gelu(value, approximate=False)


def contract_rows(left, right):
    return lax.dot_general(
        left, right, (((0,), (0,)), ((), ())), preferred_element_type=jnp.float32
    )


def contract_cols(left, right):
    return lax.dot_general(
        left, right, (((1,), (1,)), ((), ())), preferred_element_type=jnp.float32
    )


def raw_scores(query_heads, key_heads, previous, allowed, scale):
    scores = (
        jnp.einsum("sqhd,skhd->shqk", query_heads, key_heads, preferred_element_type=jnp.float32)
        * scale
    )
    scores = scores + previous.astype(jnp.float32)
    return (scores, jnp.where(allowed[None, None], scores, -1e30))


def body(
    hidden_in,
    prev_logits,
    w_query,
    w_key,
    w_value,
    w_out,
    w_inner,
    w_outer,
    b_query,
    b_value,
    b_out,
    b_inner,
    b_outer,
    gain_attn,
    shift_attn,
    gain_ffn,
    shift_ffn,
    d_output,
    d_logits,
):
    seq_count, rows, width = hidden_in.shape
    heads_here = prev_logits.shape[1]
    full_len = prev_logits.shape[3]
    local_width = w_query.shape[1]
    head_size = local_width // heads_here
    scale = head_size ** (-0.5)
    tokens = seq_count * rows
    my_ctx = lax.axis_index("ctx")
    query_pos = my_ctx * rows + jnp.arange(rows, dtype=jnp.int32)
    key_pos = jnp.arange(full_len, dtype=jnp.int32)
    allowed = (key_pos // BLOCK)[None, :] <= (query_pos // BLOCK)[:, None]
    query_full, key_full, value_full, out_full, inner_full, outer_full = (
        lax.all_gather(w_query, "fsdp", axis=0, tiled=True),
        lax.all_gather(w_key, "fsdp", axis=0, tiled=True),
        lax.all_gather(w_value, "fsdp", axis=0, tiled=True),
        lax.all_gather(w_out, "fsdp", axis=0, tiled=True),
        lax.all_gather(w_inner, "fsdp", axis=0, tiled=True),
        lax.all_gather(w_outer, "fsdp", axis=0, tiled=True),
    )
    flat = hidden_in.reshape(tokens, width)
    flat_f = flat.astype(jnp.float32)
    query = (jnp.dot(flat, query_full, preferred_element_type=jnp.float32) + b_query).astype(
        jnp.bfloat16
    )
    keys = jnp.dot(flat, key_full, preferred_element_type=jnp.float32).astype(jnp.bfloat16)
    values = (jnp.dot(flat, value_full, preferred_element_type=jnp.float32) + b_value).astype(
        jnp.bfloat16
    )
    keys_all, values_all = (
        lax.all_gather(keys.reshape(seq_count, rows, local_width), "ctx", axis=1, tiled=True),
        lax.all_gather(values.reshape(seq_count, rows, local_width), "ctx", axis=1, tiled=True),
    )
    query_heads = query.reshape(seq_count, rows, heads_here, head_size)
    key_heads = keys_all.reshape(seq_count, full_len, heads_here, head_size)
    value_heads = values_all.reshape(seq_count, full_len, heads_here, head_size)
    scores, masked = raw_scores(query_heads, key_heads, prev_logits, allowed, scale)
    new_logits = jnp.where(allowed[None, None], scores, 0.0).astype(jnp.bfloat16)
    highest = jnp.max(masked, axis=-1, keepdims=True)
    unnorm = jnp.exp(masked - highest)
    total = jnp.sum(unnorm, axis=-1, keepdims=True)
    log_total = highest + jnp.log(total)
    probs_low = (unnorm / total).astype(jnp.bfloat16)
    mixed = jnp.einsum(
        "shqk,skhd->sqhd", probs_low, value_heads, preferred_element_type=jnp.float32
    )
    attended = mixed.reshape(tokens, local_width).astype(jnp.bfloat16)
    attn_part = contract_cols(attended, out_full)
    cotangent = d_output.reshape(tokens, width).astype(jnp.float32)
    first = flat_f + lax.psum(attn_part, "tp") + b_out
    normed_f, attn_pull = jax.vjp(layer_norm, first, gain_attn, shift_attn)
    normed = normed_f.astype(jnp.bfloat16)
    inner = jnp.dot(normed, inner_full, preferred_element_type=jnp.float32) + b_inner
    act_f, gelu_pull = jax.vjp(gelu_exact, inner)
    act = act_f.astype(jnp.bfloat16)
    ffn_part = contract_cols(act, outer_full)
    second = normed.astype(jnp.float32) + lax.psum(ffn_part, "tp") + b_outer
    result_f, ffn_pull = jax.vjp(layer_norm, second, gain_ffn, shift_ffn)
    output = result_f.astype(jnp.bfloat16).reshape(seq_count, rows, width)
    grad_second, grad_gain_ffn, grad_shift_ffn = ffn_pull(cotangent)
    grad_b_outer = jnp.sum(grad_second, axis=0)
    second_low = grad_second.astype(jnp.bfloat16)
    grad_w_outer = contract_rows(second_low, act)
    grad_act = jnp.dot(second_low, outer_full, preferred_element_type=jnp.float32)
    grad_inner = gelu_pull(grad_act)[0]
    grad_b_inner = jnp.sum(grad_inner, axis=0)
    inner_low = grad_inner.astype(jnp.bfloat16)
    grad_w_inner = contract_rows(normed, inner_low)
    normed_part = contract_cols(inner_low, inner_full)
    grad_normed = lax.psum(normed_part, "tp") + grad_second
    grad_first, grad_gain_attn, grad_shift_attn = attn_pull(grad_normed)
    grad_b_out = jnp.sum(grad_first, axis=0)
    first_low = grad_first.astype(jnp.bfloat16)
    grad_w_out = contract_rows(first_low, attended)
    grad_attended = jnp.dot(first_low, out_full, preferred_element_type=jnp.float32).astype(
        jnp.bfloat16
    )
    grad_heads = grad_attended.reshape(seq_count, rows, heads_here, head_size)
    probs = jnp.exp(masked - log_total)
    probs_again = probs.astype(jnp.bfloat16)
    grad_probs = jnp.einsum(
        "sqhd,skhd->shqk", grad_heads, value_heads, preferred_element_type=jnp.float32
    )
    delta = jnp.sum(probs * grad_probs, axis=-1, keepdims=True)
    grad_scores = probs * (grad_probs - delta) + jnp.where(
        allowed[None, None], d_logits.astype(jnp.float32), 0.0
    )
    d_prev = grad_scores.astype(jnp.bfloat16)
    grad_query = (
        jnp.einsum("shqk,skhd->sqhd", d_prev, key_heads, preferred_element_type=jnp.float32) * scale
    )
    grad_keys_all = (
        jnp.einsum("shqk,sqhd->skhd", d_prev, query_heads, preferred_element_type=jnp.float32)
        * scale
    )
    grad_values_all = jnp.einsum(
        "shqk,sqhd->skhd", probs_again, grad_heads, preferred_element_type=jnp.float32
    )
    grad_keys, grad_values = (
        lax.psum_scatter(
            grad_keys_all.reshape(seq_count, full_len, local_width).astype(jnp.bfloat16),
            "ctx",
            scatter_dimension=1,
            tiled=True,
        ).astype(jnp.float32),
        lax.psum_scatter(
            grad_values_all.reshape(seq_count, full_len, local_width).astype(jnp.bfloat16),
            "ctx",
            scatter_dimension=1,
            tiled=True,
        ).astype(jnp.float32),
    )
    grad_query = grad_query.reshape(tokens, local_width)
    grad_keys = grad_keys.reshape(tokens, local_width)
    grad_values = grad_values.reshape(tokens, local_width)
    grad_b_query = jnp.sum(grad_query, axis=0)
    grad_b_value = jnp.sum(grad_values, axis=0)
    query_low = grad_query.astype(jnp.bfloat16)
    keys_low = grad_keys.astype(jnp.bfloat16)
    values_low = grad_values.astype(jnp.bfloat16)
    grad_w_query = contract_rows(flat, query_low)
    grad_w_key = contract_rows(flat, keys_low)
    grad_w_value = contract_rows(flat, values_low)
    input_part = contract_cols(query_low, query_full) + contract_cols(keys_low, key_full)
    input_part = input_part + contract_cols(values_low, value_full)
    d_hidden = (
        lax.psum(input_part.astype(jnp.bfloat16), "tp").astype(jnp.float32) + grad_first
    ).reshape(seq_count, rows, width)
    small_sums = lax.psum(
        (
            grad_b_query,
            grad_b_value,
            grad_b_inner,
            grad_b_out,
            grad_b_outer,
            grad_gain_attn,
            grad_shift_attn,
            grad_gain_ffn,
            grad_shift_ffn,
        ),
        ("fsdp", "ctx"),
    )
    sum_query, sum_value, sum_inner = (small_sums[0], small_sums[1], small_sums[2])
    sum_out, sum_outer, sum_gain_attn, sum_shift_attn, sum_gain_ffn, sum_shift_ffn = small_sums[3:]
    weight_grads = (grad_w_query, grad_w_key, grad_w_value, grad_w_out, grad_w_inner, grad_w_outer)
    weight_grads = (
        lax.psum_scatter(
            weight_grads[0].astype(jnp.bfloat16), "fsdp", scatter_dimension=0, tiled=True
        ).astype(jnp.float32),
        lax.psum_scatter(
            weight_grads[1].astype(jnp.bfloat16), "fsdp", scatter_dimension=0, tiled=True
        ).astype(jnp.float32),
        lax.psum_scatter(
            weight_grads[2].astype(jnp.bfloat16), "fsdp", scatter_dimension=0, tiled=True
        ).astype(jnp.float32),
        lax.psum_scatter(
            weight_grads[3].astype(jnp.bfloat16), "fsdp", scatter_dimension=0, tiled=True
        ).astype(jnp.float32),
        lax.psum_scatter(
            weight_grads[4].astype(jnp.bfloat16), "fsdp", scatter_dimension=0, tiled=True
        ).astype(jnp.float32),
        lax.psum_scatter(
            weight_grads[5].astype(jnp.bfloat16), "fsdp", scatter_dimension=0, tiled=True
        ).astype(jnp.float32),
    )
    weight_grads = (
        lax.psum(weight_grads[0].astype(jnp.bfloat16), "ctx").astype(jnp.float32),
        lax.psum(weight_grads[1].astype(jnp.bfloat16), "ctx").astype(jnp.float32),
        lax.psum(weight_grads[2].astype(jnp.bfloat16), "ctx").astype(jnp.float32),
        lax.psum(weight_grads[3].astype(jnp.bfloat16), "ctx").astype(jnp.float32),
        lax.psum(weight_grads[4].astype(jnp.bfloat16), "ctx").astype(jnp.float32),
        lax.psum(weight_grads[5].astype(jnp.bfloat16), "ctx").astype(jnp.float32),
    )
    return (
        output,
        new_logits,
        d_hidden,
        d_prev,
        weight_grads[0],
        weight_grads[1],
        weight_grads[2],
        weight_grads[3],
        weight_grads[4],
        weight_grads[5],
        sum_query,
        sum_value,
        sum_out,
        sum_inner,
        sum_outer,
        sum_gain_attn,
        sum_shift_attn,
        sum_gain_ffn,
        sum_shift_ffn,
    )


def solution(mesh):
    in_specs = (
        P("fsdp", "ctx", None),
        P("fsdp", "tp", "ctx", None),
        P("fsdp", "tp"),
        P("fsdp", "tp"),
        P("fsdp", "tp"),
        P("fsdp", "tp"),
        P("fsdp", "tp"),
        P("fsdp", "tp"),
        P("tp"),
        P("tp"),
        P(),
        P("tp"),
        P(),
        P(),
        P(),
        P(),
        P(),
        P("fsdp", "ctx", None),
        P("fsdp", "tp", "ctx", None),
    )
    out_specs = (
        P("fsdp", "ctx", None),
        P("fsdp", "tp", "ctx", None),
        P("fsdp", "ctx", None),
        P("fsdp", "tp", "ctx", None),
        P("fsdp", "tp"),
        P("fsdp", "tp"),
        P("fsdp", "tp"),
        P("fsdp", "tp"),
        P("fsdp", "tp"),
        P("fsdp", "tp"),
        P("tp"),
        P("tp"),
        P(),
        P("tp"),
        P(),
        P(),
        P(),
        P(),
        P(),
    )
    return jax.shard_map(body, mesh=mesh, in_specs=in_specs, out_specs=out_specs, check_vma=False)
```

profile of v0, /device:TPU:0, one launch (start us, length us, event | category | flops | bytes accessed | tf_op | source)
XLA Modules:
  0.0 1649.5 jit_solution(8693518717527014616)
XLA Ops:
  8.1 8.3 all_gather.27
  17.2 4.0 convolution_convert_fusion.1
  24.2 6.6 all_gather.24
  36.7 6.6 all_gather.26
  43.3 6.8 all_gather.29
  52.2 3.5 reshape.226
  58.7 16.1 select_reduce_fusion
  75.4 12.2 fusion.2
  89.5 12.2 fusion.40
  103.4 3.8 fusion.74
  108.6 222.5 %all-reduce.8.cloned.1.call-done = f32[2048,768]{1,0:T(8,128)} async-done(((f32[2048,768]{1,0:T(8,128)}), f32[2048,768]{1,0:T(8,128)}) %all-reduce.8.cloned.1.call-update) | async-done | bytes 6291472 | tf_op jit(solution)/shard_map/psum | solution.py:110
  331.1 3.7 fusion.72
  338.6 19.8 %multiply_convert_fusion = (bf16[2048,768]{1,0:T(8,128)(2,1)}, f32[2048,768]{1,0:T(8,128)}, f32[2048,768]{1,0:T(8,128)}) fusion(f32[768]{0:T(1024)} %param.30, bf16[2048,768]{1,0:T(8,128)(2,1)S(1)} %add_convert_fusion.3, bf16[768,768]{1,0:T(8,128)(2,1)} %all-gather.9.cloned.1.call-done), kind=kOutput, calls=%fused_computation.39 | convolution fusion | flops 2519728128 | bytes 20057088 | tf_op jit(solution)/shard_map/dot_general | solution.py:113
  358.5 7.6 fusion.75
  366.1 221.9 %all-reduce.10.cloned.1.call-done = f32[2048,768]{1,0:T(8,128)} async-done(((f32[2048,768]{1,0:T(8,128)}), f32[2048,768]{1,0:T(8,128)}) %all-reduce.10.cloned.1.call-update) | async-done | bytes 6291472 | tf_op jit(solution)/shard_map/psum | solution.py:117
  588.0 5.7 fusion.70
  598.8 4.3 fusion.69
  603.2 5.6 fusion.73
  610.5 4.5 fusion.34
  615.9 221.2 %all-reduce.12.cloned.1.call-done = f32[2048,768]{1,0:T(8,128)} async-done(((f32[2048,768]{1,0:T(8,128)}), f32[2048,768]{1,0:T(8,128)}) %all-reduce.12.cloned.1.call-update) | async-done | bytes 6291472 | tf_op jit(solution)/shard_map/psum | solution.py:130
  837.1 8.7 multiply_reduce_fusion.1
  845.8 4.2 fusion.68
  855.8 36.6 %add_convert_fusion = bf16[4,3,512,1024]{3,2,1,0:T(8,128)(2,1)} fusion(bf16[4,3,512,1024]{3,2,1,0:T(8,128)(2,1)} %param.37, f32[4,3,512,1024]{3,2,1,0:T(8,128)} %get-tuple-element.112, f32[4,3,512]{2,1,0:T(4,128)S(1)} %log_add_fusion, pred[512,1024]{1,0:T(8,128)(4,1)S(1)} %copy-done.7, bf16[4,1024,3,64]{1,3,2,0:T(8,128)(2,1)S(1)} %bitcast.151, ...), kind=kOutput, calls=%fused_computation.1 | convolution fusion | flops 1679825920 | bytes 53239808 | tf_op jit(solution)/shard_map/sub | solution.py:145
  892.3 6.9 multiply_convert_fusion.1
  899.2 36.0 %copy.77 = bf16[4,1024,192]{0,2,1:T(8,128)(2,1)} copy(bf16[4,1024,192]{1,2,0:T(8,128)(2,1)S(1)} %bitcast.139) | data formatting | bytes 3145728
  935.2 91.2 %reshape.235 = bf16[1024,768]{1,0:T(8,128)(2,1)} reshape(bf16[1024,192,4]{2,1,0:T(8,128)(2,1)} %bitcast.128) | data formatting | bytes 3145728
  1026.4 11.7 fusion.29
  1038.2 35.9 %copy.79 = bf16[4,1024,192]{0,2,1:T(8,128)(2,1)} copy(bf16[4,1024,192]{1,2,0:T(8,128)(2,1)S(1)} %bitcast.149) | data formatting | bytes 3145728
  1074.1 90.9 %reshape.237 = bf16[1024,768]{1,0:T(8,128)(2,1)} reshape(bf16[1024,192,4]{2,1,0:T(8,128)(2,1)} %bitcast.129) | data formatting | bytes 3145728
  1165.3 10.6 bitcast_convert_fusion
  1179.5 56.7 %reshape.236 = bf16[512,192,4]{2,1,0:T(8,128)(2,1)} reshape(bf16[512,768]{1,0:T(8,128)(2,1)} %reduce-scatter.25.cloned.1.call-done) | data formatting | bytes 1572864
  1236.2 23.6 %copy.72 = bf16[4,512,192]{1,2,0:T(8,128)(2,1)} copy(bf16[4,512,192]{0,2,1:T(8,128)(2,1)} %bitcast.126) | data formatting | bytes 1572864 | tf_op jit(solution)/shard_map/reduce_scatter | solution.py:160
  1262.7 56.7 %reshape.238 = bf16[512,192,4]{2,1,0:T(8,128)(2,1)} reshape(bf16[512,768]{1,0:T(8,128)(2,1)} %reduce-scatter.27.cloned.1.call-done) | data formatting | bytes 1572864
  1319.5 23.6 %copy.73 = bf16[4,512,192]{1,2,0:T(8,128)(2,1)} copy(bf16[4,512,192]{0,2,1:T(8,128)(2,1)} %bitcast.124) | data formatting | bytes 1572864 | tf_op jit(solution)/shard_map/reduce_scatter | solution.py:166
  1346.4 6.5 fusion.36
  1353.0 7.6 convolution_convert_fusion.2
  1360.8 5.0 convolution_convert_fusion.3
  1365.8 3.8 fusion.76
  1371.2 23.7 %copy.78 = bf16[4,512,192]{1,0,2:T(4,128)(2,1)S(1)} copy(bf16[4,512,192]{0,2,1:T(8,128)(2,1)} %bitcast.127) | data formatting | bytes 1572864
  1398.5 23.7 %reduce-scatter.23.cloned.1.call-done = bf16[192,768]{1,0:T(8,128)(2,1)} async-done(((bf16[768,768]{1,0:T(8,128)(2,1)}), bf16[192,768]{1,0:T(8,128)(2,1)}) %reduce-scatter.23.cloned.1.call-update) | async-done | bytes 294928 | tf_op jit(solution)/shard_map/reduce_scatter | solution.py:222
  1422.2 23.3 %reduce-scatter.19.cloned.1.call-done = bf16[192,192]{1,0:T(8,128)(2,1)} async-done(((bf16[768,192]{1,0:T(8,128)(2,1)}), bf16[192,192]{1,0:T(8,128)(2,1)}) %reduce-scatter.19.cloned.1.call-update) | async-done | bytes 73744 | tf_op jit(solution)/shard_map/reduce_scatter | solution.py:216
  1445.8 3.7 fusion.77
  1449.5 23.5 %copy.80 = bf16[4,512,192]{1,0,2:T(4,128)(2,1)S(1)} copy(bf16[4,512,192]{0,2,1:T(8,128)(2,1)} %bitcast.125) | data formatting | bytes 1572864
  1474.0 7.9 add_convert_fusion.1
  1482.4 14.8 select_convert_fusion
  1508.8 102.9 %all-reduce.14.cloned.1.call-done = bf16[2048,768]{1,0:T(8,128)(2,1)} async-done(((bf16[2048,768]{1,0:T(8,128)(2,1)}), bf16[2048,768]{1,0:T(8,128)(2,1)}) %all-reduce.14.cloned.1.call-update) | async-done | bytes 3145744 | tf_op jit(solution)/shard_map/psum | solution.py:187
  1611.6 5.9 add_reduce_fusion
  1617.5 24.7 %all-reduce = (f32[192]{0:T(256)}, f32[192]{0:T(256)}, f32[768]{0:T(1024)}, f32[768]{0:T(1024)}, f32[768]{0:T(1024)}, /*index=5*/f32[768]{0:T(1024)}, f32[768]{0:T(1024)}, f32[768]{0:T(1024)}, f32[768]{0:T(1024)}) all-reduce(f32[192]{0:T(256)S(1)} %reduce_sum.216, ...), channel_id=1, replica_groups=mesh['fsdp'=4,'ctx'=2,'tp'=4] {'fsdp','ctx'}, use_global_device_ids=true, to_apply=%region_30.31 | all-reduce | flops 5760 | bytes 46080 | tf_op jit(solution)/shard_map/psum | solution.py:189
  (220 shorter events, 66.0 us)
Async XLA Ops:
  8.0 23.5 %copy-start.2 = (bf16[4,512,768]{2,1,0:T(8,128)(2,1)S(1)}, bf16[4,512,768]{2,1,0:T(8,128)(2,1)}, u32[]{:S(2)}) copy-start(bf16[4,512,768]{2,1,0:T(8,128)(2,1)} %param.19) | copy-start | bytes 9437188
  8.0 16.2 copy-start.31
  8.0 23.5 %copy-start.55 = (f32[192]{0:T(256)S(1)}, f32[192]{0:T(256)}, u32[]{:S(2)}) copy-start(f32[192]{0:T(256)} %param.28) | copy-start | bytes 2308
  8.1 48.8 %all-gather.7.cloned.1.call-start = ((), (), s32[]{:S(2)}) async-start(), calls=%async_computation.9 | async-start | bytes 2359296 | tf_op jit(solution)/shard_map/all_gather | solution.py:91
  17.2 19.6 %copy-start.32 = (bf16[192,192]{1,0:T(8,128)(2,1)S(1)}, bf16[192,192]{1,0:T(8,128)(2,1)}, u32[]{:S(2)}) copy-start(bf16[192,192]{1,0:T(8,128)(2,1)} %param.21) | copy-start | bytes 221188
  21.2 29.0 %copy-start.56 = (f32[192]{0:T(256)S(1)}, f32[192]{0:T(256)}, u32[]{:S(2)}) copy-start(f32[192]{0:T(256)} %param.27) | copy-start | bytes 2308
  24.2 63.4 %all-gather.5.cloned.1.call-start = ((), (), s32[]{:S(2)}) async-start(), calls=%async_computation.8 | async-start | bytes 2359296 | tf_op jit(solution)/shard_map/all_gather | solution.py:92
  36.6 294.4 %all-reduce.8.cloned.1.call-start = ((), (), s32[]{:S(2)}) async-start(), calls=%async_computation.10 | async-start | bytes 12582912 | tf_op jit(solution)/shard_map/psum | solution.py:110
  58.7 16.1 copy-start.9
  58.7 16.7 %copy-start.6 = (pred[512,1024]{1,0:T(8,128)(4,1)S(1)}, pred[512,1024]{1,0:T(8,128)(4,1)}, u32[]{:S(2)}) copy-start(pred[512,1024]{1,0:T(8,128)(4,1)} %broadcast_compare_fusion) | copy-start | bytes 1572868
  89.5 12.2 copy-start.23
  107.1 223.9 %copy-start.50 = (f32[768]{0:T(1024)S(1)}, f32[768]{0:T(1024)}, u32[]{:S(2)}) copy-start(f32[768]{0:T(1024)} %param.29) | copy-start | bytes 9220
  107.2 231.5 %all-gather.9.cloned.1.call-start = ((), (), s32[]{:S(2)}) async-start(), calls=%async_computation.11 | async-start | bytes 1474560 | tf_op jit(solution)/shard_map/all_gather | solution.py:78
  107.7 250.7 %all-gather.11.cloned.1.call-start = ((), (), s32[]{:S(2)}) async-start(), calls=%async_computation.12 | async-start | bytes 1474560 | tf_op jit(solution)/shard_map/all_gather | solution.py:79
  108.3 479.7 %all-reduce.10.cloned.1.call-start = ((), (), s32[]{:S(2)}) async-start(), calls=%async_computation.13 | async-start | bytes 12582912 | tf_op jit(solution)/shard_map/psum | solution.py:117
  338.6 19.9 %copy-start.20 = (bf16[2048,768]{1,0:T(8,128)(2,1)}, bf16[2048,768]{1,0:T(8,128)(2,1)S(1)}, u32[]{:S(2)}) copy-start(bf16[2048,768]{1,0:T(8,128)(2,1)S(1)} %add_convert_fusion.3) | copy-start | bytes 9437188
  366.1 222.0 %copy-start.38 = (f32[768]{0:T(1024)S(1)}, f32[768]{0:T(1024)}, u32[]{:S(2)}) copy-start(f32[768]{0:T(1024)} %param.32) | copy-start | bytes 9220
  366.1 222.0 %copy-start.44 = (f32[768]{0:T(1024)S(1)}, f32[768]{0:T(1024)}, u32[]{:S(2)}) copy-start(f32[768]{0:T(1024)} %param.33) | copy-start | bytes 9220
  366.1 222.0 %copy-start.51 = (f32[768]{0:T(1024)S(1)}, f32[768]{0:T(1024)}, u32[]{:S(2)}) copy-start(f32[768]{0:T(1024)} %param.31) | copy-start | bytes 9220
  366.1 471.0 %all-reduce.12.cloned.1.call-start = ((), (), s32[]{:S(2)}) async-start(), calls=%async_computation.14 | async-start | bytes 12582912 | tf_op jit(solution)/shard_map/psum | solution.py:130
  603.1 234.0 %copy-start.39 = (f32[2048]{0:T(1024)}, f32[2048]{0:T(1024)S(1)}, u32[]{:S(2)}) copy-start(f32[2048]{0:T(1024)S(1)} %negate_multiply_fusion.2) | copy-start | bytes 24580
  615.1 564.4 %reduce-scatter.25.cloned.1.call-start = ((), (), s32[]{:S(2)}) async-start(), calls=%async_computation.19 | async-start | bytes 2359296
  615.9 229.9 %copy-start.34 = (f32[2048]{0:T(1024)S(1)}, f32[2048]{0:T(1024)}, u32[]{:S(2)}) copy-start(f32[2048]{0:T(1024)} %copy-done.33) | copy-start | bytes 24580
  850.1 42.2 %copy-start.35 = (f32[2048]{0:T(1024)}, f32[2048]{0:T(1024)S(1)}, u32[]{:S(2)}) copy-start(f32[2048]{0:T(1024)S(1)} %negate_multiply_fusion.1) | copy-start | bytes 24580
  855.8 36.6 %copy-start.14 = (bf16[4,512,3,64]{1,0,3,2:T(4,128)(2,1)S(1)}, bf16[4,512,3,64]{1,0,3,2:T(4,128)(2,1)}, u32[]{:S(2)}) copy-start(bf16[4,512,3,64]{1,0,3,2:T(4,128)(2,1)} %reshape.226) | copy-start | bytes 2359300
  935.2 91.2 %copy-start.27 = (bf16[4,512,3,64]{1,0,3,2:T(4,128)(2,1)S(1)}, bf16[4,512,3,64]{1,0,3,2:T(4,128)(2,1)}, u32[]{:S(2)}) copy-start(bf16[4,512,3,64]{1,0,3,2:T(4,128)(2,1)} %reshape.230) | copy-start | bytes 2359300
  1026.4 236.4 %reduce-scatter.27.cloned.1.call-start = ((), (), s32[]{:S(2)}) async-start(), calls=%async_computation.20 | async-start | bytes 2359296
  1165.0 12.6 copy-start.3
  1165.0 204.6 %reduce-scatter.29.cloned.1.call-start = ((), (), s32[]{:S(2)}) async-start(), calls=%async_computation.21 | async-start | bytes 491520
  1179.4 215.8 %reduce-scatter.31.cloned.1.call-start = ((), (), s32[]{:S(2)}) async-start(), calls=%async_computation.22 | async-start | bytes 491520
  1262.7 134.2 %reduce-scatter.33.cloned.1.call-start = ((), (), s32[]{:S(2)}) async-start(), calls=%async_computation.23 | async-start | bytes 491520
  1345.0 8.0 copy-start.40
  1346.0 52.5 %reduce-scatter.21.cloned.1.call-start = ((), (), s32[]{:S(2)}) async-start(), calls=%async_computation.17 | async-start | bytes 1474560 | tf_op jit(solution)/shard_map/reduce_scatter | solution.py:219
  1353.0 7.8 copy-start.17
  1353.0 69.2 %reduce-scatter.23.cloned.1.call-start = ((), (), s32[]{:S(2)}) async-start(), calls=%async_computation.18 | async-start | bytes 1474560 | tf_op jit(solution)/shard_map/reduce_scatter | solution.py:222
  1360.7 84.9 %reduce-scatter.19.cloned.1.call-start = ((), (), s32[]{:S(2)}) async-start(), calls=%async_computation.16 | async-start | bytes 491520 | tf_op jit(solution)/shard_map/reduce_scatter | solution.py:216
  1365.8 132.7 %all-reduce.16.cloned.1.call-start = ((), (), s32[]{:S(2)}) async-start(), calls=%async_computation.24 | async-start | bytes 1966080 | tf_op jit(solution)/shard_map/psum | solution.py:227
  1371.2 74.5 %copy-start.19 = (bf16[768,192]{1,0:T(8,128)(2,1)S(1)}, bf16[768,192]{1,0:T(8,128)(2,1)}, u32[]{:S(2)}) copy-start(bf16[768,192]{1,0:T(8,128)(2,1)} %copy-done.18) | copy-start | bytes 884740
  1445.6 166.1 %all-reduce.14.cloned.1.call-start = ((), (), s32[]{:S(2)}) async-start(), calls=%async_computation.15 | async-start | bytes 6291456 | tf_op jit(solution)/shard_map/psum | solution.py:187
  1449.5 24.5 %copy-start.26 = (bf16[768,192]{1,0:T(8,128)(2,1)S(1)}, bf16[768,192]{1,0:T(8,128)(2,1)}, u32[]{:S(2)}) copy-start(bf16[768,192]{1,0:T(8,128)(2,1)} %copy-done.25) | copy-start | bytes 884740
  1474.0 7.9 copy-start.5
  1482.4 14.8 copy-start.15
  1482.4 15.0 copy-start.13
  1508.7 108.8 %copy-start.42 = (f32[768]{0:T(1024)S(1)}, f32[768]{0:T(1024)}, u32[]{:S(2)}) copy-start(f32[768]{0:T(1024)} %get-tuple-element.78) | copy-start | bytes 9220
  1508.7 108.8 %copy-start.45 = (f32[768]{0:T(1024)S(1)}, f32[768]{0:T(1024)}, u32[]{:S(2)}) copy-start(f32[768]{0:T(1024)} %get-tuple-element.76) | copy-start | bytes 9220
  1508.7 108.8 %copy-start.46 = (f32[768]{0:T(1024)S(1)}, f32[768]{0:T(1024)}, u32[]{:S(2)}) copy-start(f32[768]{0:T(1024)} %get-tuple-element.80) | copy-start | bytes 9220
  1508.7 108.8 %copy-start.47 = (f32[768]{0:T(1024)S(1)}, f32[768]{0:T(1024)}, u32[]{:S(2)}) copy-start(f32[768]{0:T(1024)} %get-tuple-element.108) | copy-start | bytes 9220
  1508.7 108.8 %copy-start.49 = (f32[768]{0:T(1024)S(1)}, f32[768]{0:T(1024)}, u32[]{:S(2)}) copy-start(f32[768]{0:T(1024)} %get-tuple-element.116) | copy-start | bytes 9220
  (31 other events, 109.9 us)
Sparse Core Ops, SparseCore 0:
  24.3 28.1 all-gather.6
  54.5 27.1 all-gather.4
  107.3 223.7 all-reduce.7
  366.2 221.7 all-reduce.9
  615.2 221.7 all-reduce.11
  1026.5 25.0 reduce-scatter.24
  1165.2 25.0 reduce-scatter.26
  1192.7 20.7 reduce-scatter.28
  1262.8 19.3 reduce-scatter.30
  1346.1 19.3 reduce-scatter.32
  1368.1 25.7 reduce-scatter.20
  1396.4 25.7 reduce-scatter.22
  1424.7 20.7 reduce-scatter.18
  1448.6 39.4 all-reduce.15
  1490.5 121.0 all-reduce.13
Sparse Core Ops, SparseCore 1:
  109.2 18.2 all-gather.8
  128.9 17.3 all-gather.10
where the time goes:
time: 1660 us; the launch traced here: 1650 us
  waiting for transfers between devices  817 us (49%)
  local copies, waits for them, and re-layouts  504 us (30%)
  matrix products  184 us (11%)
  other arithmetic  73.5 us (4%)
  blocking collectives  52.9 us (3%)
    unnamed x145, local copies, waits for them, and re-layouts  441 us
    psum x1, waiting for transfers between devices, body(): first = flat_f + lax.psum(attn_part, 'tp') + b_out  223 us
    psum x1, waiting for transfers between devices, body(): second = normed.astype(jnp.float32) + lax.psum(ffn_part, 'tp') + b_outer  222 us
    psum x1, waiting for transfers between devices, body(): grad_normed = lax.psum(normed_part, 'tp') + grad_second  221 us
    psum x1, waiting for transfers between devices, body(): lax.psum(input_part.astype(jnp.bfloat16), 'tp').astype(jnp.float32)  103 us
    sub x1, matrix products, body(): grad_probs - delta  36.6 us
  transfers between devices with their start and end apart: 17, of which 6 were waited for; matrix products, arithmetic and copies ran while one was open for 30% of the time, Pallas kernels for 0%

commit v1 on v0

--- a/solution.py
+++ b/solution.py
@@ -107,7 +107,7 @@
     attended = mixed.reshape(tokens, local_width).astype(jnp.bfloat16)
     attn_part = contract_cols(attended, out_full)
     cotangent = d_output.reshape(tokens, width).astype(jnp.float32)
-    first = flat_f + lax.psum(attn_part, "tp") + b_out
+    first = flat_f + jnp.sum(lax.all_gather(attn_part, "tp"), axis=0) + b_out
     normed_f, attn_pull = jax.vjp(layer_norm, first, gain_attn, shift_attn)
     normed = normed_f.astype(jnp.bfloat16)
     inner = jnp.dot(normed, inner_full, preferred_element_type=jnp.float32) + b_inner

time: 1660 us -> 1890 us (1.14)
  waiting for transfers between devices: 817 us -> 1020 us
    all_gather x0 -> x1, waiting for transfers between devices: none -> 425 us  [body(): first = flat_f + jnp.sum(lax.all_gather(attn_part, 'tp'), axis=0) + b_out]
    psum x1 -> x0, waiting for transfers between devices: 223 us -> none  [body(): first = flat_f + lax.psum(attn_part, 'tp') + b_out]
    unnamed x145 -> x125, local copies, waits for them, and re-layouts: 441 us -> 440 us
  transfers between devices with their start and end apart: 17 -> 17, of which waited for: 6 -> 6; matrix products, arithmetic and copies ran while one was open for 30% -> 28% of each run, Pallas kernels for 0% -> 0%
where the time goes in v1:
time: 1890 us; the launch traced here: 1880 us
  waiting for transfers between devices  1020 us (54%)
  local copies, waits for them, and re-layouts  505 us (27%)
  matrix products  191 us (10%)
  other arithmetic  91.9 us (5%)
  blocking collectives  52.9 us (3%)
    unnamed x125, local copies, waits for them, and re-layouts  440 us
    all_gather x1, waiting for transfers between devices, body(): first = flat_f + jnp.sum(lax.all_gather(attn_part, 'tp'), axis=0) + b_out  425 us
    psum x1, waiting for transfers between devices, body(): second = normed.astype(jnp.float32) + lax.psum(ffn_part, 'tp') + b_outer  221 us
    psum x1, waiting for transfers between devices, body(): grad_normed = lax.psum(normed_part, 'tp') + grad_second  220 us
    psum x1, waiting for transfers between devices, body(): lax.psum(input_part.astype(jnp.bfloat16), 'tp').astype(jnp.float32)  103 us
  transfers between devices with their start and end apart: 17, of which 6 were waited for; matrix products, arithmetic and copies ran while one was open for 28% of the time, Pallas kernels for 0%

profile of v1, /device:TPU:0, one launch (start us, length us, event | category | flops | bytes accessed | tf_op | source)
XLA Modules:
  0.0 1875.6 jit_solution(10505046572751191598)
XLA Ops:
  7.3 8.3 all_gather.33
  16.4 4.0 convolution_convert_fusion.1
  23.4 6.6 all_gather.30
  35.9 6.6 all_gather.32
  42.5 6.8 all_gather.35
  57.9 16.0 select_reduce_fusion
  74.6 12.2 fusion.2
  88.6 12.2 fusion.41
  102.5 3.8 fusion.74
  107.7 424.9 %all-gather.15.cloned.1.call-done = f32[8192,768]{1,0:T(8,128)} async-done(((f32[2048,768]{1,0:T(8,128)}), f32[8192,768]{1,0:T(8,128)}) %all-gather.15.cloned.1.call-update) | async-done | bytes 25165840 | tf_op jit(solution)/shard_map/all_gather | solution.py:110
  532.6 12.8 reduce_sum.183
  545.4 3.9 fusion.25
  555.4 18.9 %multiply_convert_fusion = (bf16[2048,768]{1,0:T(8,128)(2,1)}, f32[2048,768]{1,0:T(8,128)}, f32[2048,768]{1,0:T(8,128)}) fusion(f32[768]{0:T(1024)} %param.30, bf16[2048,768]{1,0:T(8,128)(2,1)} %add_convert_fusion.3, bf16[768,768]{1,0:T(8,128)(2,1)} %all-gather.11.cloned.1.call-done), kind=kOutput, calls=%fused_computation.39 | convolution fusion | flops 2519728128 | bytes 20057088 | tf_op jit(solution)/shard_map/dot_general | solution.py:113
  574.3 7.4 fusion.75
  581.8 221.1 %all-reduce.7.cloned.1.call-done = f32[2048,768]{1,0:T(8,128)} async-done(((f32[2048,768]{1,0:T(8,128)}), f32[2048,768]{1,0:T(8,128)}) %all-reduce.7.cloned.1.call-update) | async-done | bytes 6291472 | tf_op jit(solution)/shard_map/psum | solution.py:117
  803.0 4.6 fusion.71
  812.6 4.3 fusion.70
  816.9 10.4 fusion.73
  829.0 4.5 fusion.35
  835.4 220.1 %all-reduce.9.cloned.1.call-done = f32[2048,768]{1,0:T(8,128)} async-done(((f32[2048,768]{1,0:T(8,128)}), f32[2048,768]{1,0:T(8,128)}) %all-reduce.9.cloned.1.call-update) | async-done | bytes 6291472 | tf_op jit(solution)/shard_map/psum | solution.py:130
  1055.5 10.6 multiply_reduce_fusion.1
  1066.1 4.7 fusion.69
  1078.8 36.7 %add_convert_fusion = bf16[4,3,512,1024]{3,2,1,0:T(8,128)(2,1)} fusion(bf16[4,3,512,1024]{3,2,1,0:T(8,128)(2,1)} %param.37, f32[4,3,512,1024]{3,2,1,0:T(8,128)} %get-tuple-element.112, f32[4,3,512]{2,1,0:T(4,128)} %log_add_fusion, pred[512,1024]{1,0:T(8,128)(4,1)} %broadcast_compare_fusion, bf16[4,1024,3,64]{1,3,2,0:T(8,128)(2,1)} %bitcast.170, ...), kind=kOutput, calls=%fused_computation.1 | convolution fusion | flops 1679825920 | bytes 53239808 | tf_op jit(solution)/shard_map/sub | solution.py:145
  1115.5 8.4 multiply_convert_fusion.1
  1123.9 36.6 %copy.77 = bf16[4,1024,192]{0,2,1:T(8,128)(2,1)} copy(bf16[4,1024,192]{1,2,0:T(8,128)(2,1)} %bitcast.158) | data formatting | bytes 3145728
  1160.4 91.1 %reshape.265 = bf16[1024,768]{1,0:T(8,128)(2,1)} reshape(bf16[1024,192,4]{2,1,0:T(8,128)(2,1)} %bitcast.146) | data formatting | bytes 3145728
  1251.6 13.1 fusion.30
  1264.7 36.3 %copy.79 = bf16[4,1024,192]{0,2,1:T(8,128)(2,1)} copy(bf16[4,1024,192]{1,2,0:T(8,128)(2,1)} %bitcast.168) | data formatting | bytes 3145728
  1301.1 90.9 %reshape.267 = bf16[1024,768]{1,0:T(8,128)(2,1)} reshape(bf16[1024,192,4]{2,1,0:T(8,128)(2,1)} %bitcast.147) | data formatting | bytes 3145728
  1392.3 10.3 bitcast_convert_fusion
  1406.2 56.7 %reshape.266 = bf16[512,192,4]{2,1,0:T(8,128)(2,1)} reshape(bf16[512,768]{1,0:T(8,128)(2,1)} %reduce-scatter.25.cloned.1.call-done) | data formatting | bytes 1572864
  1462.8 23.6 %copy.72 = bf16[4,512,192]{1,2,0:T(8,128)(2,1)} copy(bf16[4,512,192]{0,2,1:T(8,128)(2,1)} %bitcast.142) | data formatting | bytes 1572864 | tf_op jit(solution)/shard_map/reduce_scatter | solution.py:160
  1489.4 56.7 %reshape.268 = bf16[512,192,4]{2,1,0:T(8,128)(2,1)} reshape(bf16[512,768]{1,0:T(8,128)(2,1)} %reduce-scatter.27.cloned.1.call-done) | data formatting | bytes 1572864
  1546.1 23.6 %copy.73 = bf16[4,512,192]{1,2,0:T(8,128)(2,1)} copy(bf16[4,512,192]{0,2,1:T(8,128)(2,1)} %bitcast.140) | data formatting | bytes 1572864 | tf_op jit(solution)/shard_map/reduce_scatter | solution.py:166
  1573.0 6.5 fusion.37
  1579.7 7.6 convolution_convert_fusion.2
  1587.4 5.0 convolution_convert_fusion.3
  1592.5 3.8 fusion.76
  1597.9 23.7 %copy.78 = bf16[4,512,192]{1,0,2:T(4,128)(2,1)S(1)} copy(bf16[4,512,192]{0,2,1:T(8,128)(2,1)} %bitcast.143) | data formatting | bytes 1572864
  1625.1 23.9 %reduce-scatter.23.cloned.1.call-done = bf16[192,768]{1,0:T(8,128)(2,1)} async-done(((bf16[768,768]{1,0:T(8,128)(2,1)}), bf16[192,768]{1,0:T(8,128)(2,1)}) %reduce-scatter.23.cloned.1.call-update) | async-done | bytes 294928 | tf_op jit(solution)/shard_map/reduce_scatter | solution.py:222
  1649.0 23.2 %reduce-scatter.19.cloned.1.call-done = bf16[192,192]{1,0:T(8,128)(2,1)} async-done(((bf16[768,192]{1,0:T(8,128)(2,1)}), bf16[192,192]{1,0:T(8,128)(2,1)}) %reduce-scatter.19.cloned.1.call-update) | async-done | bytes 73744 | tf_op jit(solution)/shard_map/reduce_scatter | solution.py:216
  1672.4 3.7 fusion.77
  1676.1 23.5 %copy.80 = bf16[4,512,192]{1,0,2:T(4,128)(2,1)S(1)} copy(bf16[4,512,192]{0,2,1:T(8,128)(2,1)} %bitcast.141) | data formatting | bytes 1572864
  1700.6 7.9 add_convert_fusion.1
  1709.0 14.8 select_convert_fusion
  1735.4 102.9 %all-reduce.11.cloned.1.call-done = bf16[2048,768]{1,0:T(8,128)(2,1)} async-done(((bf16[2048,768]{1,0:T(8,128)(2,1)}), bf16[2048,768]{1,0:T(8,128)(2,1)}) %all-reduce.11.cloned.1.call-update) | async-done | bytes 3145744 | tf_op jit(solution)/shard_map/psum | solution.py:187
  1838.2 5.9 add_reduce_fusion
  1844.1 24.7 %all-reduce = (f32[192]{0:T(256)}, f32[192]{0:T(256)}, f32[768]{0:T(1024)}, f32[768]{0:T(1024)}, f32[768]{0:T(1024)}, /*index=5*/f32[768]{0:T(1024)}, f32[768]{0:T(1024)}, f32[768]{0:T(1024)}, f32[768]{0:T(1024)}) all-reduce(f32[192]{0:T(256)S(1)} %reduce_sum.229, ...), channel_id=1, replica_groups=mesh['fsdp'=4,'ctx'=2,'tp'=4] {'fsdp','ctx'}, use_global_device_ids=true, to_apply=%region_30.31 | all-reduce | flops 5760 | bytes 46080 | tf_op jit(solution)/shard_map/psum | solution.py:189
  (200 shorter events, 75.0 us)
Async XLA Ops:
  7.2 23.6 %copy-start.1 = (bf16[4,512,768]{2,1,0:T(8,128)(2,1)S(1)}, bf16[4,512,768]{2,1,0:T(8,128)(2,1)}, u32[]{:S(2)}) copy-start(bf16[4,512,768]{2,1,0:T(8,128)(2,1)} %param.19) | copy-start | bytes 9437188
  7.2 16.2 copy-start.26
  7.2 23.5 %copy-start.48 = (f32[192]{0:T(256)S(1)}, f32[192]{0:T(256)}, u32[]{:S(2)}) copy-start(f32[192]{0:T(256)} %param.28) | copy-start | bytes 2308
  7.2 48.8 %all-gather.9.cloned.1.call-start = ((), (), s32[]{:S(2)}) async-start(), calls=%async_computation.9 | async-start | bytes 2359296 | tf_op jit(solution)/shard_map/all_gather | solution.py:91
  16.3 19.6 %copy-start.27 = (bf16[192,192]{1,0:T(8,128)(2,1)S(1)}, bf16[192,192]{1,0:T(8,128)(2,1)}, u32[]{:S(2)}) copy-start(bf16[192,192]{1,0:T(8,128)(2,1)} %param.21) | copy-start | bytes 221188
  20.3 28.9 %copy-start.49 = (f32[192]{0:T(256)S(1)}, f32[192]{0:T(256)}, u32[]{:S(2)}) copy-start(f32[192]{0:T(256)} %param.27) | copy-start | bytes 2308
  23.4 63.4 %all-gather.7.cloned.1.call-start = ((), (), s32[]{:S(2)}) async-start(), calls=%async_computation.8 | async-start | bytes 2359296 | tf_op jit(solution)/shard_map/all_gather | solution.py:92
  35.8 496.7 %all-gather.15.cloned.1.call-start = ((), (), s32[]{:S(2)}) async-start(), calls=%async_computation.18 | async-start | bytes 31457280 | tf_op jit(solution)/shard_map/all_gather | solution.py:110
  42.5 6.8 copy-start.17
  57.9 16.0 copy-start.7
  57.9 16.7 copy-start.5
  88.6 12.2 copy-start.19
  106.3 449.1 %all-gather.11.cloned.1.call-start = ((), (), s32[]{:S(2)}) async-start(), calls=%async_computation.10 | async-start | bytes 1474560 | tf_op jit(solution)/shard_map/all_gather | solution.py:78
  106.9 467.4 %all-gather.13.cloned.1.call-start = ((), (), s32[]{:S(2)}) async-start(), calls=%async_computation.11 | async-start | bytes 1474560 | tf_op jit(solution)/shard_map/all_gather | solution.py:79
  107.5 695.5 %all-reduce.7.cloned.1.call-start = ((), (), s32[]{:S(2)}) async-start(), calls=%async_computation.12 | async-start | bytes 12582912 | tf_op jit(solution)/shard_map/psum | solution.py:117
  532.6 12.8 copy-start.23
  581.8 473.7 %all-reduce.9.cloned.1.call-start = ((), (), s32[]{:S(2)}) async-start(), calls=%async_computation.13 | async-start | bytes 12582912 | tf_op jit(solution)/shard_map/psum | solution.py:130
  816.9 10.4 copy-start.6
  816.9 10.4 copy-start.35
  816.9 12.1 copy-start.45
  833.5 572.6 %reduce-scatter.25.cloned.1.call-start = ((), (), s32[]{:S(2)}) async-start(), calls=%async_computation.19 | async-start | bytes 2359296
  1055.5 10.6 copy-start.29
  1055.5 10.6 copy-start.25
  1055.5 10.6 copy-start.33
  1160.4 91.2 %copy-start.34 = (f32[4,3,512]{2,1,0:T(4,128)S(1)}, f32[4,3,512]{2,1,0:T(4,128)}, u32[]{:S(2)}) copy-start(f32[4,3,512]{2,1,0:T(4,128)} %log_add_fusion) | copy-start | bytes 73732
  1251.5 237.9 %reduce-scatter.27.cloned.1.call-start = ((), (), s32[]{:S(2)}) async-start(), calls=%async_computation.20 | async-start | bytes 2359296
  1392.0 204.2 %reduce-scatter.29.cloned.1.call-start = ((), (), s32[]{:S(2)}) async-start(), calls=%async_computation.21 | async-start | bytes 491520
  1406.1 215.7 %reduce-scatter.31.cloned.1.call-start = ((), (), s32[]{:S(2)}) async-start(), calls=%async_computation.22 | async-start | bytes 491520
  1489.3 134.1 %reduce-scatter.33.cloned.1.call-start = ((), (), s32[]{:S(2)}) async-start(), calls=%async_computation.23 | async-start | bytes 491520
  1571.6 8.1 copy-start.36
  1572.6 52.5 %reduce-scatter.21.cloned.1.call-start = ((), (), s32[]{:S(2)}) async-start(), calls=%async_computation.16 | async-start | bytes 1474560 | tf_op jit(solution)/shard_map/reduce_scatter | solution.py:219
  1579.6 7.8 copy-start.14
  1579.6 7.8 copy-start.31
  1579.6 69.4 %reduce-scatter.23.cloned.1.call-start = ((), (), s32[]{:S(2)}) async-start(), calls=%async_computation.17 | async-start | bytes 1474560 | tf_op jit(solution)/shard_map/reduce_scatter | solution.py:222
  1587.3 5.2 copy-start.9
  1587.3 84.8 %reduce-scatter.19.cloned.1.call-start = ((), (), s32[]{:S(2)}) async-start(), calls=%async_computation.15 | async-start | bytes 491520 | tf_op jit(solution)/shard_map/reduce_scatter | solution.py:216
  1592.4 132.7 %all-reduce.13.cloned.1.call-start = ((), (), s32[]{:S(2)}) async-start(), calls=%async_computation.24 | async-start | bytes 1966080 | tf_op jit(solution)/shard_map/psum | solution.py:227
  1597.9 74.5 %copy-start.16 = (bf16[768,192]{1,0:T(8,128)(2,1)S(1)}, bf16[768,192]{1,0:T(8,128)(2,1)}, u32[]{:S(2)}) copy-start(bf16[768,192]{1,0:T(8,128)(2,1)} %copy-done.15) | copy-start | bytes 884740
  1672.2 166.1 %all-reduce.11.cloned.1.call-start = ((), (), s32[]{:S(2)}) async-start(), calls=%async_computation.14 | async-start | bytes 6291456 | tf_op jit(solution)/shard_map/psum | solution.py:187
  1676.1 24.5 %copy-start.21 = (bf16[768,192]{1,0:T(8,128)(2,1)S(1)}, bf16[768,192]{1,0:T(8,128)(2,1)}, u32[]{:S(2)}) copy-start(bf16[768,192]{1,0:T(8,128)(2,1)} %copy-done.20) | copy-start | bytes 884740
  1700.6 7.9 copy-start.4
  1709.0 14.8 copy-start.12
  1709.0 15.0 copy-start.11
  1735.3 108.8 %copy-start.38 = (f32[768]{0:T(1024)S(1)}, f32[768]{0:T(1024)}, u32[]{:S(2)}) copy-start(f32[768]{0:T(1024)} %get-tuple-element.78) | copy-start | bytes 9220
  1735.3 108.8 %copy-start.39 = (f32[768]{0:T(1024)S(1)}, f32[768]{0:T(1024)}, u32[]{:S(2)}) copy-start(f32[768]{0:T(1024)} %get-tuple-element.76) | copy-start | bytes 9220
  1735.3 108.8 %copy-start.40 = (f32[768]{0:T(1024)S(1)}, f32[768]{0:T(1024)}, u32[]{:S(2)}) copy-start(f32[768]{0:T(1024)} %get-tuple-element.80) | copy-start | bytes 9220
  1735.3 108.8 %copy-start.41 = (f32[768]{0:T(1024)S(1)}, f32[768]{0:T(1024)}, u32[]{:S(2)}) copy-start(f32[768]{0:T(1024)} %get-tuple-element.106) | copy-start | bytes 9220
  1735.3 108.8 %copy-start.44 = (f32[768]{0:T(1024)S(1)}, f32[768]{0:T(1024)}, u32[]{:S(2)}) copy-start(f32[768]{0:T(1024)} %get-tuple-element.116) | copy-start | bytes 9220
  (20 other events, 48.0 us)
Sparse Core Ops, SparseCore 0:
  23.5 28.1 all-gather.8
  53.7 27.1 all-gather.6
  106.4 426.0 all-gather.14
  534.0 15.6 all-gather.10
  551.1 17.4 all-gather.12
  581.9 221.0 all-reduce.6
  833.7 221.7 all-reduce.8
  1251.7 25.0 reduce-scatter.24
  1392.2 25.0 reduce-scatter.26
  1419.6 20.7 reduce-scatter.28
  1489.5 19.5 reduce-scatter.30
  1572.7 19.5 reduce-scatter.32
  1594.9 25.7 reduce-scatter.20
  1623.2 25.7 reduce-scatter.22
  1651.3 20.7 reduce-scatter.18
  1675.2 39.4 all-reduce.12
  1717.1 121.0 all-reduce.10
